TPU v7x, 32 devices: a whole 2x2x4 slice. The times are simulated.
32 devices in a mesh: wave: 16 (over z, x, core), rows: 2 (over y).
Axes of the slice: x: 2, y: 2, z: 4, core: 2. Of those that a mesh axis runs over, the one named last changes fastest.
Arguments:
- potential: bfloat16 [4, 128, 2048], P(None, 'rows', 'wave'), may hold values from 0 to 1
- tilt_index: int32 [32, 2], P('wave'), may hold values from -128 to 127
Outputs:
- exit_wave: bfloat16 [2, 32, 128, 2048], P(None, 'wave', 'rows')
All inputs are finite; a program needn't handle non-finite values.
Results may differ from a plain program's by a relative error of at most 0.025.
Values may be sent and summed in bfloat16 or wider, within the bound.
A program may use at most 64 MiB of HBM per device.

v0:
```python
import math

import jax
import jax.numpy as jnp
from jax import lax
from jax.sharding import PartitionSpec as P

NX = 2048
TAPS = 33
BLOCK = 128
SLICES = 4


def extended(block, sides, width):
    for axis, dim in sides:
        count = lax.axis_size(axis)
        forward = [(i, i + 1) for i in range(count - 1)]
        backward = [(target, source) for source, target in forward]
        low = lax.ppermute(
            lax.slice_in_dim(block, block.shape[dim] - width, None, axis=dim), axis, forward
        )
        high = lax.ppermute(lax.slice_in_dim(block, 0, width, axis=dim), axis, backward)
        block = jnp.concatenate([low, block, high], axis=dim)
    return block


def band_kernel(width):
    reach = TAPS // 2
    inner = jnp.arange(width + 2 * reach)[:, None]
    outer = jnp.arange(width)[None, :]
    offset = inner - outer
    valid = (offset >= 0) & (offset < TAPS)
    centred = (offset - reach).astype(jnp.float32)
    angle_val = math.pi * centred * centred / TAPS
    weight = jnp.where(valid, 1.0 / math.sqrt(TAPS), 0.0).astype(jnp.float32)
    real_part = (jnp.cos(angle_val) * weight).astype(jnp.bfloat16)
    imag_part = (jnp.sin(angle_val) * weight).astype(jnp.bfloat16)
    return jnp.stack([jnp.stack([real_part, imag_part]), jnp.stack([-imag_part, real_part])])


def column_pass(field, kernel):
    reach = TAPS // 2
    padded = jnp.pad(field, ((0, 0), (0, 0), (0, 0), (reach, reach)))
    count = field.shape[3] // BLOCK
    windows = jnp.stack(
        [padded[:, :, :, b * BLOCK : b * BLOCK + BLOCK + 2 * reach] for b in range(count)], axis=3
    )
    result = jnp.einsum("pwrbm,pqmc->qwrbc", windows, kernel, preferred_element_type=jnp.float32)
    return result.reshape(field.shape)


def row_pass(padded, kernel):
    reach = TAPS // 2
    total = padded.shape[2] - 2 * reach
    windows = jnp.stack([padded], axis=2)
    result = jnp.einsum("pwbmc,pqmr->qwbrc", windows, kernel, preferred_element_type=jnp.float32)
    return result.reshape((2, padded.shape[1], total, padded.shape[3]))


def sine_cosine(tiles):
    phase_val = 3.0 * tiles.astype(jnp.float32)
    return (jnp.cos(phase_val).astype(jnp.bfloat16), jnp.sin(phase_val).astype(jnp.bfloat16))


def per_device(potential, tilt_index):
    reach = TAPS // 2
    rows_local = potential.shape[1]
    plane_rows = rows_local * lax.axis_size("rows")
    row_block = min(BLOCK, rows_local)
    col_kernel = band_kernel(BLOCK)
    row_kernel = band_kernel(row_block)
    y_index = lax.axis_index("rows") * rows_local + jnp.arange(rows_local, dtype=jnp.int32)
    x_index = jnp.arange(NX, dtype=jnp.int32)
    y_turn = (tilt_index[:, 0:1] * y_index[None, :] % plane_rows).astype(jnp.float32) / plane_rows
    x_turn = (tilt_index[:, 1:2] * x_index[None, :] % NX).astype(jnp.float32) / NX
    angle_val = 2.0 * math.pi * (y_turn[:, :, None] + x_turn[:, None, :])
    wave = jnp.stack([jnp.cos(angle_val), jnp.sin(angle_val)]).astype(jnp.bfloat16)
    trans_re = None
    trans_im = None
    whole_plane = lax.all_gather(potential, "wave", axis=2, tiled=True)
    trans_re, trans_im = sine_cosine(whole_plane)
    for slice_num in range(SLICES):
        t_re = trans_re[slice_num]
        t_im = trans_im[slice_num]
        t_re = t_re.astype(jnp.float32)[None]
        t_im = t_im.astype(jnp.float32)[None]
        wave_re = wave[0].astype(jnp.float32)
        wave_im = wave[1].astype(jnp.float32)
        moved = jnp.stack(
            [wave_re * t_re - wave_im * t_im, wave_re * t_im + wave_im * t_re]
        ).astype(jnp.bfloat16)
        half_step = column_pass(moved, col_kernel).astype(jnp.bfloat16)
        padded = extended(half_step, (("rows", 2),), reach)
        wave = row_pass(padded, row_kernel).astype(jnp.bfloat16)
    return wave


def solution(mesh):
    placed = (P(None, "rows", "wave"), P("wave", None))
    return jax.shard_map(
        per_device,
        mesh=mesh,
        in_specs=placed,
        out_specs=P(None, "wave", "rows", None),
        check_vma=False,
    )
```

profile of v0, /device:TPU:0, one launch (start us, length us, event | category | flops | bytes accessed | tf_op | source)
XLA Modules:
  0.0 131.9 jit_solution(18336044736024458037)
XLA Ops:
  7.3 1.0 slice_reduce_fusion.1
  9.1 39.8 %all-gather.2.cloned.1.call-done = bf16[4,64,2048]{2,1,0:T(8,128)(2,1)} async-done(((bf16[4,64,128]{2,1,0:T(8,128)(2,1)}), bf16[4,64,2048]{2,1,0:T(8,128)(2,1)}) %all-gather.2.cloned.1.call-update) | async-done | bytes 1048592 | tf_op jit(solution)/shard_map/all_gather | solution.py:80
  48.9 8.4 %cosine_convert_fusion = (bf16[4,64,2048]{2,1,0:T(8,128)(2,1)S(1)}, bf16[4,64,2048]{2,1,0:T(8,128)(2,1)S(1)}) fusion(bf16[4,64,2048]{2,1,0:T(8,128)(2,1)} %all-gather.2.cloned.1.call-done), kind=kLoop, calls=%fused_computation.141 | loop fusion | flops 2097152 | bytes 3145728 | tf_op jit(solution)/shard_map/convert_element_type | solution.py:62
  57.3 1.5 %fusion.74 = (f32[64,2048]{1,0:T(8,128)S(1)}, f32[64,2048]{1,0:T(8,128)S(1)}, f32[64,2048]{1,0:T(8,128)}, f32[64,2048]{1,0:T(8,128)}, f32[64,2048]{1,0:T(8,128)}...) fusion(bf16[4,64,2048]{2,1,0:T(8,128)(2,1)S(1)} %get-tuple-element.32, ...), kind=kLoop, calls=%fused_computation.229 | loop fusion | flops 1048576 | bytes 6291456 | tf_op jit(solution)/shard_map/mul | solution.py:90
  58.9 4.3 %fusion.53 = (bf16[1,2,64,2048]{3,2,0,1:T(8,128)(2,1)S(1)}, bf16[1,2,64,2048]{3,2,0,1:T(8,128)(2,1)S(1)}) fusion(f32[64,2048]{1,0:T(8,128)S(1)} %get-tuple-element.27, f32[64,2048]{1,0:T(8,128)S(1)} %get-tuple-element.40, f32[2,2048]{1,0:T(2,128)S(1)} %fusion.153, f32[2,64]{1,0:T(2,128)S(1)} %fusion.159), kind=kLoop, calls=%fused_computation.184 | loop fusion | flops 3670016 | bytes 2114048 | tf_op jit(solution)/shard_map/convert.20
  65.0 0.8 fusion.40
  67.0 1.3 collective-permute-start.1
  68.3 4.6 %collective-permute-start = (bf16[2,2,16,2048]{3,2,0,1:T(8,128)(2,1)S(1)}, bf16[2,2,16,2048]{3,2,0,1:T(8,128)(2,1)S(1)}, u32[]{:S(2)}, u32[]{:S(2)}) collective-permute-start(bf16[2,2,16,2048]{3,2,0,1:T(8,128)(2,1)S(1)} %get-tuple-element.21), channel_id=1, source_target_pairs={{0,1},{2,3},{4,5},{6,7},{8,9},{10,11},{12,13},{14,15},{16,17},{18,... | collective-permute-start | bytes 786440 | tf_op jit(solution)/shard_map/ppermute | solution.py:19
  73.2 4.1 %collective-permute-done.1 = bf16[2,2,16,2048]{3,2,0,1:T(8,128)(2,1)S(1)} collective-permute-done((bf16[2,2,16,2048]{3,2,0,1:T(8,128)(2,1)S(1)}, bf16[2,2,16,2048]{3,2,0,1:T(8,128)(2,1)S(1)}, u32[]{:S(2)}, u32[]{:S(2)}) %collective-permute-start.1) | collective-permute-done | bytes 262176 | tf_op jit(solution)/shard_map/ppermute | solution.py:22
  77.4 1.2 collective-permute-done
  84.0 1.3 collective-permute-start.3
  85.3 4.9 %collective-permute-start.2 = (bf16[2,2,16,2048]{3,2,0,1:T(8,128)(2,1)S(1)}, bf16[2,2,16,2048]{3,2,0,1:T(8,128)(2,1)S(1)}, u32[]{:S(2)}, u32[]{:S(2)}) collective-permute-start(bf16[2,2,16,2048]{3,2,0,1:T(8,128)(2,1)S(1)} %get-tuple-element.19), channel_id=1, source_target_pairs={{0,1},{2,3},{4,5},{6,7},{8,9},{10,11},{12,13},{14,15},{16,17},{18,... | collective-permute-start | bytes 786440 | tf_op jit(solution)/shard_map/ppermute | solution.py:19
  90.2 3.1 %collective-permute-done.3 = bf16[2,2,16,2048]{3,2,0,1:T(8,128)(2,1)S(1)} collective-permute-done((bf16[2,2,16,2048]{3,2,0,1:T(8,128)(2,1)S(1)}, bf16[2,2,16,2048]{3,2,0,1:T(8,128)(2,1)S(1)}, u32[]{:S(2)}, u32[]{:S(2)}) %collective-permute-start.3) | collective-permute-done | bytes 262176 | tf_op jit(solution)/shard_map/ppermute | solution.py:22
  93.3 1.3 %collective-permute-done.2 = bf16[2,2,16,2048]{3,2,0,1:T(8,128)(2,1)S(1)} collective-permute-done((bf16[2,2,16,2048]{3,2,0,1:T(8,128)(2,1)S(1)}, bf16[2,2,16,2048]{3,2,0,1:T(8,128)(2,1)S(1)}, u32[]{:S(2)}, u32[]{:S(2)}) %collective-permute-start.2) | collective-permute-done | bytes 262176 | tf_op jit(solution)/shard_map/ppermute | solution.py:19
  99.4 1.3 collective-permute-start.5
  100.7 4.6 %collective-permute-start.4 = (bf16[2,2,16,2048]{3,2,0,1:T(8,128)(2,1)S(1)}, bf16[2,2,16,2048]{3,2,0,1:T(8,128)(2,1)S(1)}, u32[]{:S(2)}, u32[]{:S(2)}) collective-permute-start(bf16[2,2,16,2048]{3,2,0,1:T(8,128)(2,1)S(1)} %get-tuple-element.17), channel_id=1, source_target_pairs={{0,1},{2,3},{4,5},{6,7},{8,9},{10,11},{12,13},{14,15},{16,17},{18,... | collective-permute-start | bytes 786440 | tf_op jit(solution)/shard_map/ppermute | solution.py:19
  105.3 2.4 %collective-permute-done.5 = bf16[2,2,16,2048]{3,2,0,1:T(8,128)(2,1)S(1)} collective-permute-done((bf16[2,2,16,2048]{3,2,0,1:T(8,128)(2,1)S(1)}, bf16[2,2,16,2048]{3,2,0,1:T(8,128)(2,1)S(1)}, u32[]{:S(2)}, u32[]{:S(2)}) %collective-permute-start.5) | collective-permute-done | bytes 262176 | tf_op jit(solution)/shard_map/ppermute | solution.py:22
  107.8 1.4 %collective-permute-done.4 = bf16[2,2,16,2048]{3,2,0,1:T(8,128)(2,1)S(1)} collective-permute-done((bf16[2,2,16,2048]{3,2,0,1:T(8,128)(2,1)S(1)}, bf16[2,2,16,2048]{3,2,0,1:T(8,128)(2,1)S(1)}, u32[]{:S(2)}, u32[]{:S(2)}) %collective-permute-start.4) | collective-permute-done | bytes 262176 | tf_op jit(solution)/shard_map/ppermute | solution.py:19
  111.9 0.8 fusion.49
  113.9 1.3 collective-permute-start.7
  115.2 4.6 %collective-permute-start.6 = (bf16[2,2,16,2048]{3,2,0,1:T(8,128)(2,1)S(1)}, bf16[2,2,16,2048]{3,2,0,1:T(8,128)(2,1)S(1)}, u32[]{:S(2)}, u32[]{:S(2)}) collective-permute-start(bf16[2,2,16,2048]{3,2,0,1:T(8,128)(2,1)S(1)} %get-tuple-element.15), channel_id=1, source_target_pairs={{0,1},{2,3},{4,5},{6,7},{8,9},{10,11},{12,13},{14,15},{16,17},{18,... | collective-permute-start | bytes 786440 | tf_op jit(solution)/shard_map/ppermute | solution.py:19
  119.8 2.4 %collective-permute-done.7 = bf16[2,2,16,2048]{3,2,0,1:T(8,128)(2,1)S(1)} collective-permute-done((bf16[2,2,16,2048]{3,2,0,1:T(8,128)(2,1)S(1)}, bf16[2,2,16,2048]{3,2,0,1:T(8,128)(2,1)S(1)}, u32[]{:S(2)}, u32[]{:S(2)}) %collective-permute-start.7) | collective-permute-done | bytes 262176 | tf_op jit(solution)/shard_map/ppermute | solution.py:22
  122.2 1.5 %collective-permute-done.6 = bf16[2,2,16,2048]{3,2,0,1:T(8,128)(2,1)S(1)} collective-permute-done((bf16[2,2,16,2048]{3,2,0,1:T(8,128)(2,1)S(1)}, bf16[2,2,16,2048]{3,2,0,1:T(8,128)(2,1)S(1)}, u32[]{:S(2)}, u32[]{:S(2)}) %collective-permute-start.6) | collective-permute-done | bytes 262176 | tf_op jit(solution)/shard_map/ppermute | solution.py:19
  123.7 1.5 %fusion.4 = bf16[2,2,64,2048]{3,2,1,0:T(8,128)(2,1)} fusion(bf16[2,2,16,2048]{3,2,0,1:T(8,128)(2,1)S(1)} %collective-permute-done.7, bf16[2,2,64,2048]{3,2,0,1:T(8,128)(2,1)S(1)} %reshape.330, bf16[2,2,16,2048]{3,2,0,1:T(8,128)(2,1)S(1)} %collective-permute-done.6, bf16[1,2,96,64]{2,3,0,1:T(8,128)(2,1)S(1)} %get-tuple-element.36, ...), kind=kOutput, calls=%fused_computation.124 | convolution fusion | flops 206667776 | bytes 2670592 | tf_op jit(solution)/shard_map/pwbmc,pqmr->qwbrc/dot_general | solution.py:56
  (107 shorter events, 18.5 us)
Async XLA Ops:
  6.5 42.4 %all-gather.2.cloned.1.call-start = ((), (), s32[]{:S(2)}) async-start(), calls=%async_computation | async-start | bytes 1114112 | tf_op jit(solution)/shard_map/all_gather | solution.py:80
  67.0 10.3 %collective-permute-start.1 = (bf16[2,2,16,2048]{3,2,0,1:T(8,128)(2,1)S(1)}, bf16[2,2,16,2048]{3,2,0,1:T(8,128)(2,1)S(1)}, u32[]{:S(2)}, u32[]{:S(2)}) collective-permute-start(bf16[2,2,16,2048]{3,2,0,1:T(8,128)(2,1)S(1)} %get-tuple-element.22), channel_id=1, source_target_pairs={{1,0},{3,2},{5,4},{7,6},{9,8},{11,10},{13,12},{15,14},{17,16},{19,... | collective-permute-start | bytes 786440 | tf_op jit(solution)/shard_map/ppermute | solution.py:22
  68.3 10.2 %collective-permute-start = (bf16[2,2,16,2048]{3,2,0,1:T(8,128)(2,1)S(1)}, bf16[2,2,16,2048]{3,2,0,1:T(8,128)(2,1)S(1)}, u32[]{:S(2)}, u32[]{:S(2)}) collective-permute-start(bf16[2,2,16,2048]{3,2,0,1:T(8,128)(2,1)S(1)} %get-tuple-element.21), channel_id=1, source_target_pairs={{0,1},{2,3},{4,5},{6,7},{8,9},{10,11},{12,13},{14,15},{16,17},{18,... | collective-permute-start | bytes 786440 | tf_op jit(solution)/shard_map/ppermute | solution.py:19
  78.6 1.0 copy-start.2
  78.6 1.2 copy-start.3
  84.0 9.3 %collective-permute-start.3 = (bf16[2,2,16,2048]{3,2,0,1:T(8,128)(2,1)S(1)}, bf16[2,2,16,2048]{3,2,0,1:T(8,128)(2,1)S(1)}, u32[]{:S(2)}, u32[]{:S(2)}) collective-permute-start(bf16[2,2,16,2048]{3,2,0,1:T(8,128)(2,1)S(1)} %get-tuple-element.20), channel_id=1, source_target_pairs={{1,0},{3,2},{5,4},{7,6},{9,8},{11,10},{13,12},{15,14},{17,16},{19,... | collective-permute-start | bytes 786440 | tf_op jit(solution)/shard_map/ppermute | solution.py:22
  85.3 9.9 %copy-start = (f32[64,2048]{1,0:T(8,128)S(1)}, f32[64,2048]{1,0:T(8,128)}, u32[]{:S(2)}) copy-start(f32[64,2048]{1,0:T(8,128)} %get-tuple-element.29) | copy-start | bytes 1572868
  85.3 9.9 %copy-start.1 = (f32[64,2048]{1,0:T(8,128)S(1)}, f32[64,2048]{1,0:T(8,128)}, u32[]{:S(2)}) copy-start(f32[64,2048]{1,0:T(8,128)} %get-tuple-element.38) | copy-start | bytes 1572868
  85.3 9.4 %collective-permute-start.2 = (bf16[2,2,16,2048]{3,2,0,1:T(8,128)(2,1)S(1)}, bf16[2,2,16,2048]{3,2,0,1:T(8,128)(2,1)S(1)}, u32[]{:S(2)}, u32[]{:S(2)}) collective-permute-start(bf16[2,2,16,2048]{3,2,0,1:T(8,128)(2,1)S(1)} %get-tuple-element.19), channel_id=1, source_target_pairs={{0,1},{2,3},{4,5},{6,7},{8,9},{10,11},{12,13},{14,15},{16,17},{18,... | collective-permute-start | bytes 786440 | tf_op jit(solution)/shard_map/ppermute | solution.py:19
  99.4 8.3 %collective-permute-start.5 = (bf16[2,2,16,2048]{3,2,0,1:T(8,128)(2,1)S(1)}, bf16[2,2,16,2048]{3,2,0,1:T(8,128)(2,1)S(1)}, u32[]{:S(2)}, u32[]{:S(2)}) collective-permute-start(bf16[2,2,16,2048]{3,2,0,1:T(8,128)(2,1)S(1)} %get-tuple-element.18), channel_id=1, source_target_pairs={{1,0},{3,2},{5,4},{7,6},{9,8},{11,10},{13,12},{15,14},{17,16},{19,... | collective-permute-start | bytes 786440 | tf_op jit(solution)/shard_map/ppermute | solution.py:22
  100.7 8.4 %collective-permute-start.4 = (bf16[2,2,16,2048]{3,2,0,1:T(8,128)(2,1)S(1)}, bf16[2,2,16,2048]{3,2,0,1:T(8,128)(2,1)S(1)}, u32[]{:S(2)}, u32[]{:S(2)}) collective-permute-start(bf16[2,2,16,2048]{3,2,0,1:T(8,128)(2,1)S(1)} %get-tuple-element.17), channel_id=1, source_target_pairs={{0,1},{2,3},{4,5},{6,7},{8,9},{10,11},{12,13},{14,15},{16,17},{18,... | collective-permute-start | bytes 786440 | tf_op jit(solution)/shard_map/ppermute | solution.py:19
  113.9 8.3 %collective-permute-start.7 = (bf16[2,2,16,2048]{3,2,0,1:T(8,128)(2,1)S(1)}, bf16[2,2,16,2048]{3,2,0,1:T(8,128)(2,1)S(1)}, u32[]{:S(2)}, u32[]{:S(2)}) collective-permute-start(bf16[2,2,16,2048]{3,2,0,1:T(8,128)(2,1)S(1)} %get-tuple-element.16), channel_id=1, source_target_pairs={{1,0},{3,2},{5,4},{7,6},{9,8},{11,10},{13,12},{15,14},{17,16},{19,... | collective-permute-start | bytes 786440 | tf_op jit(solution)/shard_map/ppermute | solution.py:22
  115.2 8.4 %collective-permute-start.6 = (bf16[2,2,16,2048]{3,2,0,1:T(8,128)(2,1)S(1)}, bf16[2,2,16,2048]{3,2,0,1:T(8,128)(2,1)S(1)}, u32[]{:S(2)}, u32[]{:S(2)}) collective-permute-start(bf16[2,2,16,2048]{3,2,0,1:T(8,128)(2,1)S(1)} %get-tuple-element.15), channel_id=1, source_target_pairs={{0,1},{2,3},{4,5},{6,7},{8,9},{10,11},{12,13},{14,15},{16,17},{18,... | collective-permute-start | bytes 786440 | tf_op jit(solution)/shard_map/ppermute | solution.py:19
Sparse Core Ops, SparseCore 0:
  9.5 39.3 all-gather.1
where the time goes:
time: 132 us
  waiting for transfers between devices  58 us (44%)
  starting transfers between devices  23.8 us (18%)
  other arithmetic  22.7 us (17%)
  between operations  14.2 us (11%)
  local copies, waits for them, and re-layouts  7.39 us (6%)
  matrix products  5.94 us (4%)
    all_gather x1, waiting for transfers between devices, per_device(): whole_plane = lax.all_gather(potential, 'wave', axis=2, tiled=True)  39.8 us
    ppermute x4, starting transfers between devices, extended(): lax.ppermute(lax.slice_in_dim(block, block.shape[dim] - width, None, axis...  18.6 us
    ppermute x4, waiting for transfers between devices, extended(): lax.ppermute(lax.slice_in_dim(block, 0, width, axis=dim), axis, backward)  12.1 us
    convert_element_type x1, other arithmetic, sine_cosine(): jnp.cos(phase_val).astype(jnp.bfloat16)  8.45 us
    unnamed x56, other arithmetic  5.84 us
    ppermute x4, waiting for transfers between devices, extended(): lax.ppermute(lax.slice_in_dim(block, block.shape[dim] - width, None, axis...  5.42 us
    another operation x4, other arithmetic  5.27 us
    ppermute x4, starting transfers between devices, extended(): lax.ppermute(lax.slice_in_dim(block, 0, width, axis=dim), axis, backward)  5.17 us
  transfers between devices with their start and end apart: 9, of which 9 were waited for; matrix products, arithmetic and copies ran while one was open for 2% of the time, Pallas kernels for 0%

commit v1 on v0

v1 whole, which is shorter than its diff:
```python
import functools
import math

import jax
import jax.numpy as jnp
import numpy as np
from jax import lax
from jax.experimental import pallas as pl
from jax.experimental.pallas import tpu as pltpu
from jax.sharding import PartitionSpec as P

TAPS = 33
REACH = TAPS // 2
LANES = 128
GROUP = 4
MESH = pl.DeviceIdType.MESH

SIN_COEF = (9.99999997e-01, -1.66666606e-01, 8.33311822e-03, -1.98143924e-04, 2.61811836e-06)
COS_COEF = (9.99999970e-01, -4.99999341e-01, 4.16643157e-02, -1.38594940e-03, 2.32943501e-05)


def tap_parts(offset):
    centred = (offset - REACH).astype(jnp.float32)
    angle_val = math.pi * centred * centred / TAPS
    valid = (offset >= 0) & (offset < TAPS)
    weight = jnp.where(valid, 1.0 / math.sqrt(TAPS), 0.0).astype(jnp.float32)
    real_part = (jnp.cos(angle_val) * weight).astype(jnp.bfloat16)
    imag_part = (jnp.sin(angle_val) * weight).astype(jnp.bfloat16)
    return real_part, imag_part


def tile_band():
    inner = jnp.arange(LANES)[:, None]
    outer = jnp.arange(LANES)[None, :]
    beside = jnp.where(inner < LANES // 2, inner + LANES, inner - LANES)
    parts = []
    for source in (inner, beside):
        real_part, imag_part = tap_parts(source - outer + REACH)
        top = jnp.concatenate([real_part, imag_part], axis=1)
        low = jnp.concatenate([-imag_part, real_part], axis=1)
        parts.append(jnp.concatenate([top, low], axis=0))
    return jnp.stack(parts)


class Plan:
    def __init__(self, slices, rows_local, count):
        self.sides = min(count - 1, 2)
        self.rows_local, self.count, self.slices = rows_local, count, slices
        self.high = [rows_local + self.sides * REACH * (slices - s) for s in range(slices + 1)]
        self.stored = rows_local * (1 + self.sides)

    def start(self, s, r):
        if self.sides == 0:
            return 0 * r
        if self.sides == 1:
            return r * (2 * self.rows_local - self.high[s])
        return r * self.rows_local - REACH * (self.slices - s)

    def stored_offset(self, s, r):
        if self.sides == 2:
            return self.rows_local - REACH * (self.slices - s)
        return self.start(s, r)

    def row_matrix(self, s, r):
        out_row = jnp.arange(self.high[s + 1])[:, None] + self.start(s + 1, r)
        in_row = jnp.arange(self.high[s])[None, :] + self.start(s, r)
        inside = (in_row >= 0) & (in_row < self.rows_local * self.count)
        real_part, imag_part = tap_parts(jnp.where(inside, in_row - out_row + REACH, -1))
        top = jnp.concatenate([real_part, -imag_part], axis=1)
        low = jnp.concatenate([imag_part, real_part], axis=1)
        return jnp.concatenate([top, low], axis=0)


def horner(square, coefs):
    total = square * coefs[-1] + coefs[-2]
    for coef in coefs[-3::-1]:
        total = total * square + coef
    return total


def transmission(pot):
    turn = 3.0 * pot.astype(jnp.float32) - 1.5
    square = turn * turn
    sine = horner(square, SIN_COEF) * turn
    cosine = horner(square, COS_COEF)
    mid_cos, mid_sin = math.cos(1.5), math.sin(1.5)
    return cosine * mid_cos - sine * mid_sin, sine * mid_cos + cosine * mid_sin


def modulo(value, size):
    if size & (size - 1) == 0:
        return value & (size - 1)
    return lax.rem(lax.rem(value, size) + size, size)


def gather_steps(plan, column_groups, shard, full, sems):
    send1, recv1, send2, recv2, send3, recv3, own = sems
    me, r = lax.axis_index("wave"), lax.axis_index("rows")
    z, q = me // GROUP, me % GROUP
    x, c = q // 2, q % 2
    rows = plan.rows_local
    flip_x = z * GROUP + (1 - x) * 2 + c
    sibling = z * GROUP + x * 2 + (1 - c)

    def block(s, column, row_dev, trimmed):
        need = REACH * (plan.slices - s) if trimmed else rows
        start = row_dev * rows + (1 - row_dev) * (rows - need)
        return full.at[s, :, column, pl.ds(pl.multiple_of(start, REACH), need), :]

    def remote(src, dst, send, recv, wave, row):
        return pltpu.make_async_remote_copy(
            src_ref=src, dst_ref=dst, send_sem=send, recv_sem=recv, device_id=(wave, row), device_id_type=MESH
        )

    barrier = pltpu.get_barrier_semaphore()
    others = [((z + d) % column_groups * GROUP + q, r) for d in range(1, column_groups)]
    peers = others + [(flip_x, r), (me, 1 - r), (flip_x, 1 - r), (sibling, r)]
    for peer in peers:
        pl.semaphore_signal(barrier, inc=1, device_id=peer, device_id_type=MESH)
    pl.semaphore_wait(barrier, len(peers))

    first, second, third, local = [], [], [], []
    for s in range(plan.slices):
        place = full.at[s, z, q, pl.ds(pl.multiple_of(r * rows, rows), rows), :]
        local.append(pltpu.make_async_copy(shard.at[s], place, own.at[s]))
        first.append([
            remote(shard.at[s], place, send1.at[s, d], recv1.at[s, d], *others[d])
            for d in range(column_groups - 1)
        ])
        mine, mine_cut = block(s, q, r, False), block(s, q, r, True)
        second.append([
            remote(mine, mine, send2.at[s, 0], recv2.at[s, 0], flip_x, r),
            remote(mine_cut, mine_cut, send2.at[s, 1], recv2.at[s, 1], me, 1 - r),
            remote(mine_cut, mine_cut, send2.at[s, 2], recv2.at[s, 2], flip_x, 1 - r),
        ])
        held = [
            mine,
            block(s, (1 - x) * 2 + c, r, False),
            block(s, q, 1 - r, True),
            block(s, (1 - x) * 2 + c, 1 - r, True),
        ]
        third.append([
            remote(held[k], held[k], send3.at[s, k], recv3.at[s, k], sibling, r) for k in range(4)
        ])
    return local, first, second, third


def device_kernel(plan, waves, gather, tilt, shard, band, *rest):
    slices = plan.slices
    row_mats, out = rest[:slices], rest[slices]
    scratch = rest[slices + 1 :]
    r = lax.axis_index("rows")
    if gather:
        full, moved, col_turn, row_turn = scratch[:4]
    else:
        full = shard
        moved, col_turn, row_turn = scratch[:3]
    column_groups = full.shape[1]
    tiles = column_groups * GROUP
    plane_rows = plan.rows_local * plan.count

    if gather:
        local, first, second, third = gather_steps(plan, column_groups, shard, full, scratch[4:])
        for s in range(slices):
            for copy in first[s]:
                copy.start()
            local[s].start()

    def relay_columns(s):
        if gather:
            for copy in first[s]:
                copy.wait_recv()
            local[s].wait()
            for copy in second[s]:
                copy.start()
            third[s][0].start()

    def relay_sibling(s):
        if gather:
            for k in range(3):
                second[s][k].wait_recv()
                third[s][k + 1].start()

    def arrive(s):
        if gather:
            for copy in third[s]:
                copy.wait_recv()

    for b in range(waves):
        column = lax.broadcasted_iota(jnp.int32, (tiles, LANES), 0) * LANES
        column = column + lax.broadcasted_iota(jnp.int32, (tiles, LANES), 1)
        size = tiles * LANES
        turn = modulo(tilt[b, 1] * column, size).astype(jnp.float32) * (2.0 * math.pi / size)
        col_turn[b, 0] = jnp.cos(turn)
        col_turn[b, 1] = jnp.sin(turn)
        row = lax.broadcasted_iota(jnp.int32, (plan.high[0], LANES), 0) + plan.start(0, r)
        turn = modulo(tilt[b, 0] * row, plane_rows).astype(jnp.float32) * (2.0 * math.pi / plane_rows)
        row_turn[b, 0] = jnp.cos(turn)
        row_turn[b, 1] = jnp.sin(turn)
    for half in range(2):
        for edge in (0, tiles + 1):
            moved[half, edge] = jnp.zeros(moved.shape[2:], moved.dtype)

    def transmit(s, group, lane, source):
        high = plan.high[s]
        offset = plan.stored_offset(s, r)
        for k in range(high // REACH):
            at = offset + k * REACH
            if not isinstance(at, int):
                at = pl.multiple_of(at, REACH)
            t_re, t_im = transmission(full[s, group, lane, pl.ds(at, REACH), :])
            for b in range(waves):
                w_re, w_im = source(k, b)
                to = moved.at[s % 2, group * GROUP + lane + 1, pl.ds(b * high + k * REACH, REACH)]
                to[:, :LANES] = (w_re * t_re - w_im * t_im).astype(jnp.bfloat16)
                to[:, LANES:] = (w_re * t_im + w_im * t_re).astype(jnp.bfloat16)

    for s in range(slices):
        relay_columns(s)
    relay_sibling(0)
    arrive(0)

    def begin(group, carry):
        for lane in range(GROUP):
            tile = group * GROUP + lane

            def source(k, b):
                c_re, c_im = col_turn[b, 0, pl.ds(tile, 1), :], col_turn[b, 1, pl.ds(tile, 1), :]
                span = pl.ds(k * REACH, REACH)
                r_re, r_im = row_turn[b, 0, span, :], row_turn[b, 1, span, :]
                return r_re * c_re - r_im * c_im, r_re * c_im + r_im * c_re

            transmit(0, group, lane, source)
        return carry

    lax.fori_loop(0, column_groups, begin, 0)

    for s in range(slices):
        high, low = plan.high[s], plan.high[s + 1]
        if s + 1 < slices:
            relay_sibling(s + 1)
            arrive(s + 1)

        def advance(group, carry):
            which = lax.broadcasted_iota(jnp.int32, (waves * high, 2 * LANES), 1) % LANES < LANES // 2
            for lane in range(GROUP):
                tile = group * GROUP + lane
                span = pl.ds(0, waves * high)
                beside = jnp.where(which, moved[s % 2, tile + 2, span], moved[s % 2, tile, span])
                half_step = jnp.dot(moved[s % 2, tile + 1, span], band[0], preferred_element_type=jnp.float32)
                half_step += jnp.dot(beside, band[1], preferred_element_type=jnp.float32)
                half_step = half_step.astype(jnp.bfloat16)
                stacked = jnp.concatenate(
                    [
                        jnp.concatenate(
                            [half_step[b * high : (b + 1) * high, p * LANES : (p + 1) * LANES] for b in range(waves)],
                            axis=1,
                        )
                        for p in range(2)
                    ],
                    axis=0,
                )
                result = jnp.dot(row_mats[s][...], stacked, preferred_element_type=jnp.float32)
                if s + 1 < slices:

                    def source(k, b):
                        span_b = slice(b * LANES, (b + 1) * LANES)
                        at = k * REACH
                        return result[at : at + REACH, span_b], result[low + at : low + at + REACH, span_b]

                    transmit(s + 1, group, lane, source)
                else:
                    columns = pl.ds(pl.multiple_of(tile * LANES, LANES), LANES)
                    for p in range(2):
                        for b in range(waves):
                            part = result[p * low : (p + 1) * low, b * LANES : (b + 1) * LANES]
                            out[p, b, :, columns] = part.astype(jnp.bfloat16)
            return carry

        lax.fori_loop(0, column_groups, advance, 0)

    if gather:
        for s in range(slices):
            for copy in first[s] + second[s] + third[s]:
                copy.wait_send()


def per_device(potential, tilt_index):
    slices, rows_local, width = potential.shape
    waves = tilt_index.shape[0]
    across, count = lax.axis_size("wave"), lax.axis_size("rows")
    plan = Plan(slices, rows_local, count)
    r = lax.axis_index("rows")
    tiles = width * across // LANES
    gather = count == 2 and width == LANES and across % GROUP == 0
    source = potential
    if not gather:
        plane = lax.all_gather(potential, "wave", axis=2, tiled=True)
        if plan.sides:
            up = [(i, i + 1) for i in range(count - 1)]
            above = lax.ppermute(plane, "rows", up)
            below = lax.ppermute(plane, "rows", [(b, a) for a, b in up])
            if plan.sides == 2:
                plane = jnp.concatenate([above, plane, below], axis=1)
            else:
                plane = jnp.concatenate(
                    [jnp.where(r == 0, plane, above), jnp.where(r == 0, below, plane)], axis=1
                )
        plane = plane.reshape(slices, plan.stored, tiles // GROUP, GROUP, LANES)
        source = plane.transpose(0, 2, 3, 1, 4)
    row_mats = [plan.row_matrix(s, r) for s in range(slices)]
    vmem = pl.BlockSpec(memory_space=pltpu.VMEM)
    scratch = [
        pltpu.VMEM((2, tiles + 2, waves * plan.high[0], 2 * LANES), jnp.bfloat16),
        pltpu.VMEM((waves, 2, tiles, LANES), jnp.float32),
        pltpu.VMEM((waves, 2, plan.high[0], LANES), jnp.float32),
    ]
    params = {}
    if gather:
        groups = across // GROUP
        scratch = [pltpu.VMEM((slices, groups, GROUP, plan.stored, LANES), jnp.bfloat16)] + scratch
        for size in (groups - 1, groups - 1, 3, 3, 4, 4):
            scratch.append(pltpu.SemaphoreType.DMA((slices, size)))
        scratch.append(pltpu.SemaphoreType.DMA((slices,)))
        params = dict(collective_id=0, has_side_effects=True)
    return pl.pallas_call(
        functools.partial(device_kernel, plan, waves, gather),
        out_shape=jax.ShapeDtypeStruct((2, waves, rows_local, width * across), jnp.bfloat16),
        in_specs=[pl.BlockSpec(memory_space=pltpu.SMEM)] + [vmem] * (2 + slices),
        out_specs=vmem,
        scratch_shapes=scratch,
        compiler_params=pltpu.CompilerParams(vmem_limit_bytes=60 * 1024 * 1024, **params),
    )(tilt_index, source, tile_band(), *row_mats)


def solution(mesh):
    placed = (P(None, "rows", "wave"), P("wave", None))
    return jax.shard_map(
        per_device,
        mesh=mesh,
        in_specs=placed,
        out_specs=P(None, "wave", "rows", None),
        check_vma=False,
    )
```

time: 132 us -> 52.5 us (0.40)
  waiting for transfers between devices: 58 us -> 0 us
  Pallas kernels: 0 us -> 43 us
  starting transfers between devices: 23.8 us -> 0 us
  other arithmetic: 22.7 us -> 6.89 us
  between operations: 14.2 us -> 0.13 us
  matrix products: 5.94 us -> 0 us
  local copies, waits for them, and re-layouts: 7.39 us -> 2.3 us
    pallas_call x0 -> x1, Pallas kernels: none -> 43 us  [per_device(): pl.pallas_call(functools.partial(device_kernel, plan, waves, gather), out...]
    all_gather x1 -> x0, waiting for transfers between devices: 39.8 us -> none  [per_device(): whole_plane = lax.all_gather(potential, 'wave', axis=2, tiled=True)]
    ppermute x8 -> x0, starting transfers between devices: 23.8 us -> none  [the longest x4 18.6 us: extended(): lax.ppermute(lax.slice_in_dim(block, block.shape[dim] - width, None, axis...]
    ppermute x8 -> x0, waiting for transfers between devices: 17.5 us -> none  [the longest x4 12.1 us: extended(): lax.ppermute(lax.slice_in_dim(block, 0, width, axis=dim), axis, backward)]
    convert_element_type x3 -> x6, other arithmetic: 8.94 us -> 1.65 us  [the longest x5 1.38 us: tap_parts(): imag_part = (jnp.sin(angle_val) * weight).astype(jnp.bfloat16)]
    dot_general x8 -> x0, matrix products: 5.94 us -> none  [the longest x4 3.02 us: column_pass(): jnp.einsum('pwrbm,pqmc->qwrbc', windows, kernel, preferred_element_type=j...]
    unnamed x56 -> x0, other arithmetic: 5.84 us -> none
    another operation x10 -> x3, other arithmetic: 5.7 us -> 0.76 us  [tile_band(): return jnp.stack(parts)]
  transfers between devices with their start and end apart: 9 -> 0, of which waited for: 9 -> 0; matrix products, arithmetic and copies ran while one was open for 2% -> 0% of each run, Pallas kernels for 0% -> 0%
where the time goes in v1:
time: 52.5 us; the launch traced here: 52.3 us
  Pallas kernels  43 us (82%)
  other arithmetic  6.89 us (13%)
  local copies, waits for them, and re-layouts  2.3 us (4%)
    pallas_call x1, Pallas kernels, per_device(): pl.pallas_call(functools.partial(device_kernel, plan, waves, gather), out...  43 us
    concatenate x4, other arithmetic, row_matrix(): return jnp.concatenate([top, low], axis=0)  2.84 us
    unnamed x1, local copies, waits for them, and re-layouts  2.3 us
    convert_element_type x5, other arithmetic, tap_parts(): imag_part = (jnp.sin(angle_val) * weight).astype(jnp.bfloat16)  1.38 us

profile of v1, /device:TPU:0, one launch (start us, length us, event | category | flops | bytes accessed | tf_op | source)
XLA Modules:
  0.0 52.3 jit_solution(12089629929635326034)
XLA Ops:
  0.1 0.2 fusion.43
  0.3 0.2 fusion.42
  0.6 0.3 fusion.41
  0.8 0.3 fusion.40
  1.1 0.2 fusion.33
  1.4 0.7 %maximum_maximum_fusion.3.rest_3_ = bf16[128,160]{1,0:T(8,128)(2,1)} fusion(bf16[64,80]{1,0:T(8,128)(2,1)S(1)} %get-tuple-element.6, bf16[64,80]{1,0:T(8,128)(2,1)S(1)} %get-tuple-element.5, bf16[64,80]{1,0:T(8,128)(2,1)S(1)} %fusion.43), kind=kLoop, calls=%fused_computation.22 | loop fusion | flops 163840 | bytes 71680 | tf_op jit(solution)/shard_map/concatenate | solution.py:71
  2.1 0.3 fusion.39
  2.4 0.3 fusion.38
  2.7 0.2 fusion.27
  2.9 0.7 %maximum_maximum_fusion.2.rest_2_ = bf16[160,192]{1,0:T(8,128)(2,1)} fusion(bf16[80,96]{1,0:T(8,128)(2,1)S(1)} %get-tuple-element.8, bf16[80,96]{1,0:T(8,128)(2,1)S(1)} %get-tuple-element.7, bf16[80,96]{1,0:T(8,128)(2,1)S(1)} %fusion.42), kind=kLoop, calls=%fused_computation.12 | loop fusion | flops 245760 | bytes 107520 | tf_op jit(solution)/shard_map/concatenate | solution.py:71
  3.6 0.3 fusion.21
  3.9 0.7 %maximum_maximum_fusion.1.rest_1_ = bf16[192,224]{1,0:T(8,128)(2,1)} fusion(bf16[96,112]{1,0:T(8,128)(2,1)S(1)} %get-tuple-element.10, bf16[96,112]{1,0:T(8,128)(2,1)S(1)} %get-tuple-element.9, bf16[96,112]{1,0:T(8,128)(2,1)S(1)} %fusion.41), kind=kLoop, calls=%fused_computation.4 | loop fusion | flops 344064 | bytes 150528 | tf_op jit(solution)/shard_map/concatenate | solution.py:71
  4.7 0.3 fusion.15
  5.0 0.7 %maximum_maximum_fusion.rest_0_ = bf16[224,256]{1,0:T(8,128)(2,1)} fusion(bf16[112,128]{1,0:T(8,128)(2,1)S(1)} %get-tuple-element.12, bf16[112,128]{1,0:T(8,128)(2,1)S(1)} %get-tuple-element.11, bf16[112,128]{1,0:T(8,128)(2,1)S(1)} %fusion.40), kind=kLoop, calls=%fused_computation.3 | loop fusion | flops 458752 | bytes 200704 | tf_op jit(solution)/shard_map/concatenate | solution.py:71
  5.6 0.3 fusion.3
  6.0 0.3 fusion
  6.3 0.7 %pad_maximum_fusion.band = bf16[2,256,256]{2,1,0:T(8,128)(2,1)} fusion(bf16[1,256,256]{2,1,0:T(8,128)(2,1)S(1)} %maximum_bitcast_fusion.1, bf16[1,256,256]{2,1,0:T(8,128)(2,1)S(1)} %maximum_bitcast_fusion), kind=kLoop, calls=%fused_computation | loop fusion | flops 131072 | bytes 524288 | tf_op jit(solution)/shard_map/stack | solution.py:42
  7.0 43.0 %shard_map.28 = bf16[2,2,64,2048]{3,2,1,0:T(8,128)(2,1)} custom-call(s32[2,2]{1,0:T(2,128)} %tilt.1, bf16[4,64,128]{2,1,0:T(8,128)(2,1)} %shard.1, bf16[2,256,256]{2,1,0:T(8,128)(2,1)} %pad_maximum_fusion.band, bf16[224,256]{1,0:T(8,128)(2,1)} %maximum_maximum_fusion.rest_0_, bf16[192,224]{1,0:T(8,128)(2,1)} %maximum_maximum_fusion.1.rest_1_, ...), custom_call_target="tpu_custom_call" | custom-call | tf_op jit(solution)/shard_map/pallas_call | solution.py:326
  50.0 2.3 %copy.4 = bf16[2,2,64,2048]{3,2,1,0:T(8,128)(2,1)} copy(bf16[2,2,64,2048]{3,2,1,0:T(8,128)(2,1)} %shard_map.28) | data formatting | bytes 2097152
  (11 shorter events, 0.1 us)

commit v2 on v1

--- a/solution.py
+++ b/solution.py
@@ -15,31 +15,32 @@
 GROUP = 4
 MESH = pl.DeviceIdType.MESH
 
+MIDDLE = 1.5
 SIN_COEF = (9.99999997e-01, -1.66666606e-01, 8.33311822e-03, -1.98143924e-04, 2.61811836e-06)
 COS_COEF = (9.99999970e-01, -4.99999341e-01, 4.16643157e-02, -1.38594940e-03, 2.32943501e-05)
 
 
-def tap_parts(offset):
-    centred = (offset - REACH).astype(jnp.float32)
-    angle_val = math.pi * centred * centred / TAPS
+def tap_parts(offset, np=np):
+    centred = (offset - REACH).astype(np.float32)
+    angle_val = np.float32(math.pi) * centred * centred / np.float32(TAPS)
     valid = (offset >= 0) & (offset < TAPS)
-    weight = jnp.where(valid, 1.0 / math.sqrt(TAPS), 0.0).astype(jnp.float32)
-    real_part = (jnp.cos(angle_val) * weight).astype(jnp.bfloat16)
-    imag_part = (jnp.sin(angle_val) * weight).astype(jnp.bfloat16)
+    weight = np.where(valid, 1.0 / math.sqrt(TAPS), 0.0).astype(np.float32)
+    real_part = (np.cos(angle_val) * weight).astype(jnp.bfloat16)
+    imag_part = (np.sin(angle_val) * weight).astype(jnp.bfloat16)
     return real_part, imag_part
 
 
 def tile_band():
-    inner = jnp.arange(LANES)[:, None]
-    outer = jnp.arange(LANES)[None, :]
-    beside = jnp.where(inner < LANES // 2, inner + LANES, inner - LANES)
+    inner = np.arange(LANES)[:, None]
+    outer = np.arange(LANES)[None, :]
+    beside = np.where(inner < LANES // 2, inner + LANES, inner - LANES)
     parts = []
     for source in (inner, beside):
         real_part, imag_part = tap_parts(source - outer + REACH)
-        top = jnp.concatenate([real_part, imag_part], axis=1)
-        low = jnp.concatenate([-imag_part, real_part], axis=1)
-        parts.append(jnp.concatenate([top, low], axis=0))
-    return jnp.stack(parts)
+        top = np.concatenate([real_part, imag_part], axis=1)
+        low = np.concatenate([-imag_part, real_part], axis=1)
+        parts.append(np.concatenate([top, low], axis=0))
+    return np.concatenate(parts, axis=0)
 
 
 class Plan:
@@ -61,14 +62,14 @@
             return self.rows_local - REACH * (self.slices - s)
         return self.start(s, r)
 
-    def row_matrix(self, s, r):
-        out_row = jnp.arange(self.high[s + 1])[:, None] + self.start(s + 1, r)
-        in_row = jnp.arange(self.high[s])[None, :] + self.start(s, r)
+    def row_matrix(self, s, r, np=np):
+        out_row = np.arange(self.high[s + 1])[:, None] + self.start(s + 1, r)
+        in_row = np.arange(self.high[s])[None, :] + self.start(s, r)
         inside = (in_row >= 0) & (in_row < self.rows_local * self.count)
-        real_part, imag_part = tap_parts(jnp.where(inside, in_row - out_row + REACH, -1))
-        top = jnp.concatenate([real_part, -imag_part], axis=1)
-        low = jnp.concatenate([imag_part, real_part], axis=1)
-        return jnp.concatenate([top, low], axis=0)
+        real_part, imag_part = tap_parts(np.where(inside, in_row - out_row + REACH, -1), np)
+        top = np.concatenate([real_part, -imag_part], axis=1)
+        low = np.concatenate([imag_part, real_part], axis=1)
+        return np.concatenate([top, low], axis=0)
 
 
 def horner(square, coefs):
@@ -79,12 +80,9 @@
 
 
 def transmission(pot):
-    turn = 3.0 * pot.astype(jnp.float32) - 1.5
+    turn = 3.0 * pot.astype(jnp.float32) - MIDDLE
     square = turn * turn
-    sine = horner(square, SIN_COEF) * turn
-    cosine = horner(square, COS_COEF)
-    mid_cos, mid_sin = math.cos(1.5), math.sin(1.5)
-    return cosine * mid_cos - sine * mid_sin, sine * mid_cos + cosine * mid_sin
+    return horner(square, COS_COEF), horner(square, SIN_COEF) * turn
 
 
 def modulo(value, size):
@@ -151,20 +149,20 @@
     scratch = rest[slices + 1 :]
     r = lax.axis_index("rows")
     if gather:
-        full, moved, col_turn, row_turn = scratch[:4]
+        full, moved, halves, col_turn, row_turn = scratch[:5]
     else:
         full = shard
-        moved, col_turn, row_turn = scratch[:3]
+        moved, halves, col_turn, row_turn = scratch[:4]
     column_groups = full.shape[1]
     tiles = column_groups * GROUP
     plane_rows = plan.rows_local * plan.count
 
     if gather:
-        local, first, second, third = gather_steps(plan, column_groups, shard, full, scratch[4:])
+        local, first, second, third = gather_steps(plan, column_groups, shard, full, scratch[5:])
         for s in range(slices):
-            for copy in first[s]:
-                copy.start()
             local[s].start()
+        for copy in first[0]:
+            copy.start()
 
     def relay_columns(s):
         if gather:
@@ -174,6 +172,8 @@
             for copy in second[s]:
                 copy.start()
             third[s][0].start()
+            for copy in first[s + 1] if s + 1 < slices else []:
+                copy.start()
 
     def relay_sibling(s):
         if gather:
@@ -195,6 +195,7 @@
         col_turn[b, 1] = jnp.sin(turn)
         row = lax.broadcasted_iota(jnp.int32, (plan.high[0], LANES), 0) + plan.start(0, r)
         turn = modulo(tilt[b, 0] * row, plane_rows).astype(jnp.float32) * (2.0 * math.pi / plane_rows)
+        turn = turn + slices * MIDDLE
         row_turn[b, 0] = jnp.cos(turn)
         row_turn[b, 1] = jnp.sin(turn)
     for half in range(2):
@@ -215,9 +216,9 @@
                 to[:, :LANES] = (w_re * t_re - w_im * t_im).astype(jnp.bfloat16)
                 to[:, LANES:] = (w_re * t_im + w_im * t_re).astype(jnp.bfloat16)
 
-    for s in range(slices):
-        relay_columns(s)
+    relay_columns(0)
     relay_sibling(0)
+    relay_columns(1)
     arrive(0)
 
     def begin(group, carry):
@@ -235,49 +236,74 @@
 
     lax.fori_loop(0, column_groups, begin, 0)
 
+    def column_pass(s, group):
+        rows = waves * plan.high[s]
+        tile = group * GROUP
+
+        def tiles_from(first_tile):
+            return moved[s % 2, pl.ds(first_tile, GROUP), pl.ds(0, rows)].reshape(GROUP * rows, 2 * LANES)
+
+        lane = lax.broadcasted_iota(jnp.int32, (GROUP * rows, 2 * LANES), 1) % LANES
+        beside = jnp.where(lane < LANES // 2, tiles_from(tile + 2), tiles_from(tile))
+        window = jnp.concatenate([tiles_from(tile + 1), beside], axis=1)
+        half_step = jnp.dot(window, band[...], preferred_element_type=jnp.float32).astype(jnp.bfloat16)
+        halves[group % 2, :, pl.ds(0, rows)] = half_step.reshape(GROUP, rows, 2 * LANES)
+
+    def row_pass(s, group):
+        high, low = plan.high[s], plan.high[s + 1]
+        matrix = row_mats[s][r if plan.count <= 2 else 0]
+        for lane in range(GROUP):
+            stacked = jnp.concatenate(
+                [
+                    jnp.concatenate(
+                        [
+                            halves[group % 2, lane, pl.ds(b * high, high), pl.ds(p * LANES, LANES)]
+                            for b in range(waves)
+                        ],
+                        axis=1,
+                    )
+                    for p in range(2)
+                ],
+                axis=0,
+            )
+            result = jnp.dot(matrix, stacked, preferred_element_type=jnp.float32)
+            if s + 1 < slices:
+
+                def source(k, b):
+                    span_b = slice(b * LANES, (b + 1) * LANES)
+                    at = k * REACH
+                    return result[at : at + REACH, span_b], result[low + at : low + at + REACH, span_b]
+
+                transmit(s + 1, group, lane, source)
+            else:
+                start = (group * GROUP + lane) * LANES
+                columns = pl.ds(start if isinstance(start, int) else pl.multiple_of(start, LANES), LANES)
+                for p in range(2):
+                    for b in range(waves):
+                        part = result[p * low : (p + 1) * low, b * LANES : (b + 1) * LANES]
+                        out[p, b, :, columns] = part.astype(jnp.bfloat16)
+
+    last = column_groups - 1
+    relay_sibling(1)
+    relay_columns(2)
+    arrive(1)
+    column_pass(0, 0)
     for s in range(slices):
-        high, low = plan.high[s], plan.high[s + 1]
+
+        def advance(group, carry):
+            column_pass(s, group + 1)
+            row_pass(s, group)
+            return carry
+
+        lax.fori_loop(0, last, advance, 0)
+        row_pass(s, last)
         if s + 1 < slices:
-            relay_sibling(s + 1)
-            arrive(s + 1)
-
-        def advance(group, carry):
-            which = lax.broadcasted_iota(jnp.int32, (waves * high, 2 * LANES), 1) % LANES < LANES // 2
-            for lane in range(GROUP):
-                tile = group * GROUP + lane
-                span = pl.ds(0, waves * high)
-                beside = jnp.where(which, moved[s % 2, tile + 2, span], moved[s % 2, tile, span])
-                half_step = jnp.dot(moved[s % 2, tile + 1, span], band[0], preferred_element_type=jnp.float32)
-                half_step += jnp.dot(beside, band[1], preferred_element_type=jnp.float32)
-                half_step = half_step.astype(jnp.bfloat16)
-                stacked = jnp.concatenate(
-                    [
-                        jnp.concatenate(
-                            [half_step[b * high : (b + 1) * high, p * LANES : (p + 1) * LANES] for b in range(waves)],
-                            axis=1,
-                        )
-                        for p in range(2)
-                    ],
-                    axis=0,
-                )
-                result = jnp.dot(row_mats[s][...], stacked, preferred_element_type=jnp.float32)
-                if s + 1 < slices:
-
-                    def source(k, b):
-                        span_b = slice(b * LANES, (b + 1) * LANES)
-                        at = k * REACH
-                        return result[at : at + REACH, span_b], result[low + at : low + at + REACH, span_b]
-
-                    transmit(s + 1, group, lane, source)
-                else:
-                    columns = pl.ds(pl.multiple_of(tile * LANES, LANES), LANES)
-                    for p in range(2):
-                        for b in range(waves):
-                            part = result[p * low : (p + 1) * low, b * LANES : (b + 1) * LANES]
-                            out[p, b, :, columns] = part.astype(jnp.bfloat16)
-            return carry
-
-        lax.fori_loop(0, column_groups, advance, 0)
+            column_pass(s + 1, 0)
+        if s + 2 < slices:
+            relay_sibling(s + 2)
+            if s + 3 < slices:
+                relay_columns(s + 3)
+            arrive(s + 2)
 
     if gather:
         for s in range(slices):
@@ -308,10 +334,14 @@
                 )
         plane = plane.reshape(slices, plan.stored, tiles // GROUP, GROUP, LANES)
         source = plane.transpose(0, 2, 3, 1, 4)
-    row_mats = [plan.row_matrix(s, r) for s in range(slices)]
+    if count <= 2:
+        row_mats = [jnp.asarray(np.stack([plan.row_matrix(s, k) for k in range(count)])) for s in range(slices)]
+    else:
+        row_mats = [plan.row_matrix(s, r, jnp)[None] for s in range(slices)]
     vmem = pl.BlockSpec(memory_space=pltpu.VMEM)
     scratch = [
         pltpu.VMEM((2, tiles + 2, waves * plan.high[0], 2 * LANES), jnp.bfloat16),
+        pltpu.VMEM((2, GROUP, waves * plan.high[0], 2 * LANES), jnp.bfloat16),
         pltpu.VMEM((waves, 2, tiles, LANES), jnp.float32),
         pltpu.VMEM((waves, 2, plan.high[0], LANES), jnp.float32),
     ]
@@ -330,7 +360,7 @@
         out_specs=vmem,
         scratch_shapes=scratch,
         compiler_params=pltpu.CompilerParams(vmem_limit_bytes=60 * 1024 * 1024, **params),
-    )(tilt_index, source, tile_band(), *row_mats)
+    )(tilt_index, source, jnp.asarray(tile_band()), *row_mats)
 
 
 def solution(mesh):

time: 52.5 us -> 38.2 us (0.73)
  Pallas kernels: 43 us -> 35.6 us
  other arithmetic: 6.89 us -> 0 us
    pallas_call x1, Pallas kernels: 43 us -> 35.6 us  [per_device(): pl.pallas_call(functools.partial(device_kernel, plan, waves, gather), out...]
    concatenate x4 -> x0, other arithmetic: 2.84 us -> none  [row_matrix(): return jnp.concatenate([top, low], axis=0)]
    convert_element_type x6 -> x0, other arithmetic: 1.65 us -> none  [the longest x5 1.38 us: tap_parts(): imag_part = (jnp.sin(angle_val) * weight).astype(jnp.bfloat16)]
    neg x6 -> x0, other arithmetic: 1.59 us -> none  [the longest x4 1.01 us: row_matrix(): top = jnp.concatenate([real_part, -imag_part], axis=1)]
    another operation x3 -> x0, other arithmetic: 0.76 us -> none  [tile_band(): return jnp.stack(parts)]
where the time goes in v2:
time: 38.2 us; the launch traced here: 37.9 us
  Pallas kernels  35.6 us (93%)
  local copies, waits for them, and re-layouts  2.3 us (6%)
    pallas_call x1, Pallas kernels, per_device(): pl.pallas_call(functools.partial(device_kernel, plan, waves, gather), out...  35.6 us
    unnamed x1, local copies, waits for them, and re-layouts  2.3 us

profile of v2, /device:TPU:0, one launch (start us, length us, event | category | flops | bytes accessed | tf_op | source)
XLA Modules:
  0.0 37.9 jit_solution(3986027824943484596)
XLA Ops:
  0.0 35.6 %shard_map.73 = bf16[2,2,64,2048]{3,2,1,0:T(8,128)(2,1)} custom-call(s32[2,2]{1,0:T(2,128)} %tilt.1, bf16[4,64,128]{2,1,0:T(8,128)(2,1)} %shard.1, bf16[512,256]{1,0:T(8,128)(2,1)} %constant.14.clone.band, bf16[2,224,256]{2,1,0:T(8,128)(2,1)} %constant.10.clone.rest_0_, bf16[2,192,224]{2,1,0:T(8,128)(2,1)} %constant.11.clone.rest_1_, ...), custom_call_target="tpu_custom_call" | custom-call | tf_op jit(solution)/shard_map/pallas_call | solution.py:356
  35.6 2.3 %copy.9 = bf16[2,2,64,2048]{3,2,1,0:T(8,128)(2,1)} copy(bf16[2,2,64,2048]{3,2,1,0:T(8,128)(2,1)} %shard_map.73) | data formatting | bytes 2097152

commit v3 on v2

--- a/solution.py
+++ b/solution.py
@@ -112,7 +112,7 @@
 
     barrier = pltpu.get_barrier_semaphore()
     others = [((z + d) % column_groups * GROUP + q, r) for d in range(1, column_groups)]
-    peers = others + [(flip_x, r), (me, 1 - r), (flip_x, 1 - r), (sibling, r)]
+    peers = others + [(flip_x, r), (me, 1 - r), (sibling, r)]
     for peer in peers:
         pl.semaphore_signal(barrier, inc=1, device_id=peer, device_id_type=MESH)
     pl.semaphore_wait(barrier, len(peers))
@@ -126,16 +126,18 @@
             for d in range(column_groups - 1)
         ])
         mine, mine_cut = block(s, q, r, False), block(s, q, r, True)
+        beyond_cut = block(s, (1 - x) * 2 + c, r, True)
         second.append([
             remote(mine, mine, send2.at[s, 0], recv2.at[s, 0], flip_x, r),
             remote(mine_cut, mine_cut, send2.at[s, 1], recv2.at[s, 1], me, 1 - r),
-            remote(mine_cut, mine_cut, send2.at[s, 2], recv2.at[s, 2], flip_x, 1 - r),
+            remote(beyond_cut, beyond_cut, send2.at[s, 2], recv2.at[s, 2], me, 1 - r),
         ])
+        beyond = (1 - x) * 2 + c
         held = [
             mine,
-            block(s, (1 - x) * 2 + c, r, False),
+            block(s, beyond, r, False),
             block(s, q, 1 - r, True),
-            block(s, (1 - x) * 2 + c, 1 - r, True),
+            block(s, beyond, 1 - r, True),
         ]
         third.append([
             remote(held[k], held[k], send3.at[s, k], recv3.at[s, k], sibling, r) for k in range(4)
@@ -143,11 +145,19 @@
     return local, first, second, third
 
 
-def device_kernel(plan, waves, gather, tilt, shard, band, *rest):
+def device_kernel(plan, waves, gather, tilt, shard, band_given, *rest):
     slices = plan.slices
-    row_mats, out = rest[:slices], rest[slices]
-    scratch = rest[slices + 1 :]
+    mats_given, out = rest[:slices], rest[slices]
+    row_mats = rest[slices + 1 : 2 * slices + 1]
+    band, sent, load_sems, out_sems = rest[2 * slices + 1 : 2 * slices + 5]
+    scratch = rest[2 * slices + 5 :]
     r = lax.axis_index("rows")
+    variant = r if plan.count <= 2 else 0
+    loads = [pltpu.make_async_copy(band_given, band, load_sems.at[slices])]
+    for s in range(slices):
+        loads.append(pltpu.make_async_copy(mats_given[s].at[variant], row_mats[s], load_sems.at[s]))
+    for copy in loads:
+        copy.start()
     if gather:
         full, moved, halves, col_turn, row_turn = scratch[:5]
     else:
@@ -160,24 +170,28 @@
     if gather:
         local, first, second, third = gather_steps(plan, column_groups, shard, full, scratch[5:])
         for s in range(slices):
+            for copy in first[s]:
+                copy.start()
             local[s].start()
-        for copy in first[0]:
-            copy.start()
 
     def relay_columns(s):
         if gather:
             for copy in first[s]:
                 copy.wait_recv()
             local[s].wait()
-            for copy in second[s]:
-                copy.start()
+            second[s][0].start()
+            second[s][1].start()
             third[s][0].start()
-            for copy in first[s + 1] if s + 1 < slices else []:
-                copy.start()
-
-    def relay_sibling(s):
+
+    def relay_across(s):
         if gather:
-            for k in range(3):
+            second[s][0].wait_recv()
+            second[s][2].start()
+            third[s][1].start()
+
+    def relay_rows(s):
+        if gather:
+            for k in (1, 2):
                 second[s][k].wait_recv()
                 third[s][k + 1].start()
 
@@ -217,8 +231,12 @@
                 to[:, LANES:] = (w_re * t_im + w_im * t_re).astype(jnp.bfloat16)
 
     relay_columns(0)
-    relay_sibling(0)
     relay_columns(1)
+    relay_across(0)
+    relay_columns(2)
+    relay_columns(3)
+    relay_across(1)
+    relay_rows(0)
     arrive(0)
 
     def begin(group, carry):
@@ -234,7 +252,11 @@
             transmit(0, group, lane, source)
         return carry
 
-    lax.fori_loop(0, column_groups, begin, 0)
+    half = column_groups // 2
+    lax.fori_loop(0, half, begin, 0)
+    relay_across(2)
+    relay_rows(1)
+    lax.fori_loop(half, column_groups, begin, 0)
 
     def column_pass(s, group):
         rows = waves * plan.high[s]
@@ -249,9 +271,15 @@
         half_step = jnp.dot(window, band[...], preferred_element_type=jnp.float32).astype(jnp.bfloat16)
         halves[group % 2, :, pl.ds(0, rows)] = half_step.reshape(GROUP, rows, 2 * LANES)
 
+    def store_of(group):
+        start = group * GROUP * LANES
+        start = start if isinstance(start, int) else pl.multiple_of(start, LANES)
+        place = out.at[:, :, :, pl.ds(start, GROUP * LANES)]
+        return pltpu.make_async_copy(sent.at[group], place, out_sems.at[group])
+
     def row_pass(s, group):
         high, low = plan.high[s], plan.high[s + 1]
-        matrix = row_mats[s][r if plan.count <= 2 else 0]
+        matrix = row_mats[s][...]
         for lane in range(GROUP):
             stacked = jnp.concatenate(
                 [
@@ -276,18 +304,20 @@
 
                 transmit(s + 1, group, lane, source)
             else:
-                start = (group * GROUP + lane) * LANES
-                columns = pl.ds(start if isinstance(start, int) else pl.multiple_of(start, LANES), LANES)
+                columns = pl.ds(lane * LANES, LANES)
                 for p in range(2):
                     for b in range(waves):
                         part = result[p * low : (p + 1) * low, b * LANES : (b + 1) * LANES]
-                        out[p, b, :, columns] = part.astype(jnp.bfloat16)
+                        sent[group, p, b, :, columns] = part.astype(jnp.bfloat16)
+        if s + 1 == slices:
+            store_of(group).start()
 
     last = column_groups - 1
-    relay_sibling(1)
-    relay_columns(2)
+    for copy in loads:
+        copy.wait()
+    column_pass(0, 0)
+    relay_across(3)
     arrive(1)
-    column_pass(0, 0)
     for s in range(slices):
 
         def advance(group, carry):
@@ -295,16 +325,20 @@
             row_pass(s, group)
             return carry
 
-        lax.fori_loop(0, last, advance, 0)
+        if s + 2 < slices:
+            lax.fori_loop(0, half, advance, 0)
+            relay_rows(s + 2)
+            lax.fori_loop(half, last, advance, 0)
+        else:
+            lax.fori_loop(0, last, advance, 0)
         row_pass(s, last)
         if s + 1 < slices:
             column_pass(s + 1, 0)
         if s + 2 < slices:
-            relay_sibling(s + 2)
-            if s + 3 < slices:
-                relay_columns(s + 3)
             arrive(s + 2)
 
+    for group in range(column_groups):
+        store_of(group).wait()
     if gather:
         for s in range(slices):
             for copy in first[s] + second[s] + third[s]:
@@ -339,6 +373,15 @@
     else:
         row_mats = [plan.row_matrix(s, r, jnp)[None] for s in range(slices)]
     vmem = pl.BlockSpec(memory_space=pltpu.VMEM)
+    anywhere = pl.BlockSpec(memory_space=pl.ANY)
+    high = plan.high
+    always = [pltpu.VMEM((2 * high[s + 1], 2 * high[s]), jnp.bfloat16) for s in range(slices)]
+    always += [
+        pltpu.VMEM((4 * LANES, 2 * LANES), jnp.bfloat16),
+        pltpu.VMEM((tiles // GROUP, 2, waves, rows_local, GROUP * LANES), jnp.bfloat16),
+        pltpu.SemaphoreType.DMA((slices + 1,)),
+        pltpu.SemaphoreType.DMA((tiles // GROUP,)),
+    ]
     scratch = [
         pltpu.VMEM((2, tiles + 2, waves * plan.high[0], 2 * LANES), jnp.bfloat16),
         pltpu.VMEM((2, GROUP, waves * plan.high[0], 2 * LANES), jnp.bfloat16),
@@ -356,9 +399,9 @@
     return pl.pallas_call(
         functools.partial(device_kernel, plan, waves, gather),
         out_shape=jax.ShapeDtypeStruct((2, waves, rows_local, width * across), jnp.bfloat16),
-        in_specs=[pl.BlockSpec(memory_space=pltpu.SMEM)] + [vmem] * (2 + slices),
-        out_specs=vmem,
-        scratch_shapes=scratch,
+        in_specs=[pl.BlockSpec(memory_space=pltpu.SMEM), vmem] + [anywhere] * (1 + slices),
+        out_specs=anywhere,
+        scratch_shapes=always + scratch,
         compiler_params=pltpu.CompilerParams(vmem_limit_bytes=60 * 1024 * 1024, **params),
     )(tilt_index, source, jnp.asarray(tile_band()), *row_mats)
 

time: 38.2 us -> 34.7 us (0.908)
  Pallas kernels: 35.6 us -> 32.2 us
    pallas_call x1, Pallas kernels: 35.6 us -> 32.2 us  [per_device(): pl.pallas_call(functools.partial(device_kernel, plan, waves, gather), out...]
where the time goes in v3:
time: 34.7 us; the launch traced here: 34.5 us
  Pallas kernels  32.2 us (93%)
  local copies, waits for them, and re-layouts  2.3 us (7%)
    pallas_call x1, Pallas kernels, per_device(): pl.pallas_call(functools.partial(device_kernel, plan, waves, gather), out...  32.2 us
    unnamed x1, local copies, waits for them, and re-layouts  2.3 us

profile of v3, /device:TPU:0, one launch (start us, length us, event | category | flops | bytes accessed | tf_op | source)
XLA Modules:
  0.0 34.5 jit_solution(1982005010734134993)
XLA Ops:
  0.0 32.2 %shard_map.73 = bf16[2,2,64,2048]{3,2,1,0:T(8,128)(2,1)} custom-call(s32[2,2]{1,0:T(2,128)} %tilt.1, bf16[4,64,128]{2,1,0:T(8,128)(2,1)} %shard.1, bf16[512,256]{1,0:T(8,128)(2,1)} %constant.14.clone.band_given, bf16[2,224,256]{2,1,0:T(8,128)(2,1)} %constant.10.clone.rest_0_, bf16[2,192,224]{2,1,0:T(8,128)(2,1)} %constant.11.clone.rest_1_, ...), custom_call_target="tpu_custom_call" | custom-call | tf_op jit(solution)/shard_map/pallas_call | solution.py:399
  32.2 2.3 %copy.9 = bf16[2,2,64,2048]{3,2,1,0:T(8,128)(2,1)} copy(bf16[2,2,64,2048]{3,2,1,0:T(8,128)(2,1)} %shard_map.73) | data formatting | bytes 2097152
